TPU v7x, 512 devices: a whole 4x4x16 slice. The times are simulated.
512 devices in a mesh: tm: 32 (over x, z_lo), height: 8 (over z_hi, y), dp: 2 (over core).
Axes of the slice: x: 4, y: 4, z: 16 (z_hi: 2, z_lo: 8; z = z_hi * 8 + z_lo), core: 2. Of those that a mesh axis runs over, the one named last changes fastest.
Arguments:
- frames_in: bfloat16 [2, 128, 32, 48, 256], P('dp', 'tm', 'height'), may hold values from -6 to 6
- cotangent: bfloat16 [2, 128, 32, 48, 256], P('dp', 'tm', 'height'), may hold values from -6 to 6
- w_spatial: bfloat16 [3, 3, 256, 256], replicated, may hold values from -0.125 to 0.125
- w_temporal: bfloat16 [3, 256, 256], replicated, may hold values from -0.21875 to 0.21875
Outputs:
- decoded: bfloat16 [2, 128, 32, 48, 256], P('dp', 'tm', 'height')
- input_grad: bfloat16 [2, 128, 32, 48, 256], P('dp', 'tm', 'height')
- spatial_grad: bfloat16 [3, 3, 256, 256], replicated
- temporal_grad: bfloat16 [3, 256, 256], replicated
All inputs are finite; a program needn't handle non-finite values.
Results may differ from a plain program's by a relative error of at most 0.0061.
Values may be sent and summed in bfloat16 or wider, within the bound.
No kernel may reach another device: no remote copies, remote signals or barrier semaphores. Data moves between devices by JAX's collectives and lax.ppermute only.
A program may use at most 64 MiB of HBM per device.

v0:
```python
import math
import jax
import jax.numpy as jnp
from jax import lax
from jax.sharding import PartitionSpec as P


def extended(x, sides, width):
    for axis, dim in sides:
        count, length = (lax.axis_size(axis), x.shape[dim])
        up = [(i, (i + 1) % count) for i in range(count - 1)]
        down = [(j, i) for i, j in up]
        last = lax.slice_in_dim(x, length - width, length, axis=dim)
        initial = lax.slice_in_dim(x, 0, width, axis=dim)
        before = lax.ppermute(last, axis, up)
        after = lax.ppermute(initial, axis, down)
        x = jnp.concatenate([before, x, after], axis=dim)
    return x


def from_behind(block, axis, distance):
    devices = range(lax.axis_size(axis))
    route = [(i - distance, i) for i in devices if i - distance in devices]
    return lax.ppermute(block, axis, route)


def silu_slope(values):
    sigmoid_value = jax.nn.sigmoid(values)
    return sigmoid_value * (1.0 + values * (1.0 - sigmoid_value))


def forward_taps(padded, row_count, col_count):
    pieces = [
        padded[:, row_tap : row_tap + row_count, col_tap : col_tap + col_count]
        for row_tap in range(3)
        for col_tap in range(3)
    ]
    return jnp.concatenate(pieces, axis=-1)


def backward_taps(padded, row_count, col_count):
    pieces = [
        padded[:, 2 - row_tap : 2 - row_tap + row_count, 2 - col_tap : 2 - col_tap + col_count]
        for row_tap in range(3)
        for col_tap in range(3)
    ]
    return jnp.concatenate(pieces, axis=-1)


def frame_taps(source, frame_count):
    return jnp.concatenate(
        [source[shift_tap : shift_tap + frame_count] for shift_tap in range(3)], axis=-1
    )


def flat_dot(left_side, right_side):
    return jnp.dot(
        left_side.reshape(-1, left_side.shape[-1]), right_side, preferred_element_type=jnp.float32
    )


def local(frames_in, cotangent, w_spatial, w_temporal):
    inputs = frames_in[0]
    upstream = cotangent[0]
    frame_count, row_count, col_count, channels = inputs.shape
    spatial_flat = w_spatial.reshape(9 * channels, channels)
    temporal_flat = w_temporal.reshape(3 * channels, channels)
    spatial_back = jnp.concatenate(
        [w_spatial[row_tap, col_tap].T for row_tap in range(3) for col_tap in range(3)], axis=0
    )
    temporal_back = jnp.concatenate([w_temporal[2].T, w_temporal[1].T, w_temporal[0].T], axis=0)
    first_shard = lax.axis_index("tm") == 0
    inputs_prev = from_behind(inputs[frame_count - 2 :], "tm", 1)
    upstream_next = from_behind(upstream[:2], "tm", -1)
    local_both = extended(jnp.concatenate([inputs, upstream], axis=-1), (("height", 1),), 1)
    rim_both = extended(jnp.concatenate([inputs_prev, upstream_next], axis=-1), (("height", 1),), 1)

    def spatial_forward(block):
        activ = jax.nn.silu(block.astype(jnp.float32)).astype(jnp.bfloat16)
        taps = forward_taps(jnp.pad(activ, ((0, 0), (0, 0), (1, 1), (0, 0))), row_count, col_count)
        out = flat_dot(taps, spatial_flat).astype(jnp.bfloat16)
        return (taps, out.reshape(block.shape[0], row_count, col_count, channels))

    activ_taps, spatial_out = spatial_forward(local_both[..., :channels])
    unused, spatial_rim = spatial_forward(rim_both[..., :channels])
    repeated = jnp.broadcast_to(spatial_out[:1], (2,) + spatial_out.shape[1:])
    earlier = jnp.where(first_shard, repeated, spatial_rim)
    padded_frames = jnp.concatenate([earlier, spatial_out], axis=0)
    frame_stack = frame_taps(padded_frames, frame_count).reshape(-1, 3 * channels)
    temporal_out = jnp.dot(frame_stack, temporal_flat, preferred_element_type=jnp.float32).reshape(
        inputs.shape
    )
    decoded = (inputs.astype(jnp.float32) + temporal_out).astype(jnp.bfloat16)

    def frame_gradient(source):
        rows = source.shape[1]
        part = flat_dot(frame_taps(source, frame_count), temporal_back)
        first_up = source[0].reshape(-1, channels)
        second_up = source[1].reshape(-1, channels)
        fold = jnp.dot(first_up, w_temporal[0].T, preferred_element_type=jnp.float32)
        fold = fold + jnp.dot(first_up, w_temporal[1].T, preferred_element_type=jnp.float32)
        fold = fold + jnp.dot(second_up, w_temporal[0].T, preferred_element_type=jnp.float32)
        part = part.reshape(frame_count, rows * col_count, channels)
        part = part.at[0].add(jnp.where(first_shard, fold, 0.0))
        return part.astype(jnp.bfloat16).reshape(frame_count, rows, col_count, channels)

    frame_grad = frame_gradient(jnp.concatenate([upstream, upstream_next], axis=0))
    up_rows = jnp.concatenate([local_both[..., channels:], rim_both[..., channels:]], axis=0)
    edge_grad = frame_gradient(jnp.stack([up_rows[:, 0], up_rows[:, row_count + 1]], axis=1))
    frame_grad_full = jnp.concatenate([edge_grad[:, :1], frame_grad, edge_grad[:, 1:]], axis=1)
    grad_pad = jnp.pad(frame_grad_full, ((0, 0), (0, 0), (1, 1), (0, 0)))
    act_grad = flat_dot(backward_taps(grad_pad, row_count, col_count), spatial_back)
    act_grad = act_grad.reshape(inputs.shape)
    input_grad = (
        upstream.astype(jnp.float32) + silu_slope(inputs.astype(jnp.float32)) * act_grad
    ).astype(jnp.bfloat16)
    cell_count = (
        frame_count
        * lax.axis_size("tm")
        * row_count
        * lax.axis_size("height")
        * col_count
        * lax.axis_size("dp")
    )
    grad_scale = 1.0 / math.sqrt(cell_count)
    contract = (((0,), (0,)), ((), ()))
    local_taps = activ_taps.reshape(-1, 9 * channels)
    spatial_term = lax.dot_general(
        local_taps, frame_grad.reshape(-1, channels), contract, preferred_element_type=jnp.float32
    )
    temporal_term = lax.dot_general(
        frame_stack, upstream.reshape(-1, channels), contract, preferred_element_type=jnp.float32
    )
    spatial_sum, temporal_sum = lax.psum(
        (spatial_term * grad_scale, temporal_term * grad_scale), ("tm", "height", "dp")
    )
    spatial_grad = spatial_sum.astype(jnp.bfloat16).reshape(3, 3, channels, channels)
    temporal_grad = temporal_sum.astype(jnp.bfloat16).reshape(3, channels, channels)
    return (decoded[None], input_grad[None], spatial_grad, temporal_grad)


def solution(mesh):
    return jax.shard_map(
        local,
        mesh=mesh,
        in_specs=(
            P("dp", "tm", "height", None, None),
            P("dp", "tm", "height", None, None),
            P(),
            P(),
        ),
        out_specs=(
            P("dp", "tm", "height", None, None),
            P("dp", "tm", "height", None, None),
            P(),
            P(),
        ),
        check_vma=False,
    )
```

profile of v0, /device:TPU:2, one launch (start us, length us, event | category | flops | bytes accessed | tf_op | source)
XLA Modules:
  0.0 259.6 jit_solution(6937136790871638325)
XLA Ops:
  0.7 1.7 slice_bitcast_fusion
  2.3 13.1 %collective-permute-start.3 = (bf16[2,4,48,256]{3,2,1,0:T(8,128)(2,1)}, bf16[2,4,48,256]{3,2,1,0:T(8,128)(2,1)S(1)}, u32[]{:S(2)}, u32[]{:S(2)}) collective-permute-start(bf16[2,4,48,256]{3,2,1,0:T(8,128)(2,1)} %slice_bitcast_fusion), channel_id=1, source_target_pairs={{16,0},{32,16},{48,32},{64,48},{80,64},{96,80},{112,96},{128,112},... | collective-permute-start | bytes 589832 | tf_op jit(solution)/shard_map/ppermute | solution.py:24
  15.5 1.6 slice_bitcast_fusion.1
  17.1 2.0 collective-permute-start.2
  19.1 1.8 pad_maximum_fusion.8
  20.9 3.5 %collective-permute-start = (bf16[4,1,48,512]{3,2,1,0:T(8,128)(2,1)}, bf16[4,1,48,512]{3,2,1,0:T(8,128)(2,1)S(1)}, u32[]{:S(2)}, u32[]{:S(2)}) collective-permute-start(bf16[4,1,48,512]{3,2,1,0:T(8,128)(2,1)} %get-tuple-element.39), channel_id=1, source_target_pairs={{0,2},{2,4},{4,6},{6,8},{8,10},{10,12},{12,14},{1,3},{3,5},{5,7},{... | collective-permute-start | bytes 589832 | tf_op jit(solution)/shard_map/ppermute | solution.py:15
  24.4 1.3 collective-permute-start.1
  25.8 0.2 fusion.75
  26.0 0.2 convolution_add_fusion.2
  26.2 0.1 fusion.92
  26.3 0.1 copy.33
  26.4 0.1 copy.32
  26.5 0.1 copy.31
  26.6 0.1 copy.30
  26.7 0.1 copy.29
  26.8 0.1 copy.28
  26.9 0.1 copy.27
  27.0 0.1 copy.26
  27.1 0.1 copy.25
  27.4 1.0 copy-done.12
  28.4 0.1 copy.22
  28.5 0.1 copy.23
  28.7 0.1 copy.24
  28.8 4.5 %collective-permute-done.2 = bf16[2,4,48,256]{3,2,1,0:T(8,128)(2,1)} collective-permute-done((bf16[2,4,48,256]{3,2,1,0:T(8,128)(2,1)}, bf16[2,4,48,256]{3,2,1,0:T(8,128)(2,1)}, u32[]{:S(2)}, u32[]{:S(2)}) %collective-permute-start.2) | collective-permute-done | bytes 196640 | tf_op jit(solution)/shard_map/ppermute | solution.py:24
  33.3 0.9 constant_dynamic-update-slice_fusion.1
  34.3 3.5 %collective-permute-start.4 = (bf16[2,1,48,512]{3,2,1,0:T(8,128)(2,1)S(1)}, bf16[2,1,48,512]{3,2,1,0:T(8,128)(2,1)S(1)}, u32[]{:S(2)}, u32[]{:S(2)}) collective-permute-start(bf16[2,1,48,512]{3,2,1,0:T(8,128)(2,1)S(1)} %get-tuple-element.50), channel_id=1, source_target_pairs={{0,2},{2,4},{4,6},{6,8},{8,10},{10,12},{12,14},{1,3},{3,5},{5,7},{... | collective-permute-start | bytes 294920 | tf_op jit(solution)/shard_map/ppermute | solution.py:15
  37.8 1.3 collective-permute-start.5
  39.1 0.1 fusion.57
  39.1 0.5 fusion.15
  39.7 0.2 fusion.71
  40.0 0.7 copy-done.3
  40.6 1.0 pad_maximum_fusion
  41.7 0.4 fusion.9
  42.1 0.1 fusion.51
  42.2 0.1 fusion.52
  42.3 0.1 fusion.53
  42.5 0.1 fusion.54
  42.6 0.1 fusion.55
  42.8 0.1 fusion.56
  42.9 1.1 convolution_multiply_fusion
  44.1 0.1 copy-done.5
  44.2 1.1 convolution_convert_fusion
  45.3 0.1 pad_maximum_fusion.1
  45.4 0.2 fusion.46
  45.6 0.4 copy-done.6
  46.0 0.5 slice-done
  46.6 0.2 fusion.78
  46.8 0.2 convolution_add_fusion.4
  47.0 0.4 copy-done.9
  47.4 0.1 copy-done.11
  47.5 0.3 fusion.64
  47.8 0.2 fusion.32
  48.5 0.6 convolution_convert_fusion.1
  49.1 0.3 fusion.42
  49.4 0.1 slice_dynamic-update-slice_fusion.5
  49.6 0.1 slice_dynamic-update-slice_fusion.3
  49.8 0.1 slice_dynamic-update-slice_fusion.1
  50.0 0.6 slice-done.1
  50.7 0.2 copy-done.7
  50.9 0.1 fusion.58
  50.9 1.2 fusion.4
  52.2 1.4 convolution_multiply_fusion.1
  53.5 1.9 fusion.5
  55.5 204.1 %all-reduce.5 = (bf16[2304,256]{1,0:T(8,128)(2,1)}, bf16[768,256]{1,0:T(8,128)(2,1)}) all-reduce(f32[2304,256]{1,0:T(8,128)S(1)} %convolution_multiply_fusion, f32[768,256]{1,0:T(8,128)} %convolution_multiply_fusion.1), channel_id=1, replica_groups=mesh['tm'=32,'height'=8,'dp'=2] {'tm','height','dp'}, use_global_device_ids=true, to_apply=%region_0.1 | all-reduce | flops 786432 | bytes 4718592 | tf_op jit(solution)/shard_map/psum | solution.py:134
  (68 shorter events, 1.1 us)
Async XLA Ops:
  0.6 25.1 %copy-start = (bf16[1,4,4,48,256]{4,3,2,1,0:T(8,128)(2,1)S(1)}, bf16[1,4,4,48,256]{4,3,2,1,0:T(8,128)(2,1)}, u32[]{:S(2)}) copy-start(bf16[1,4,4,48,256]{4,3,2,1,0:T(8,128)(2,1)} %param.9) | copy-start | bytes 1179652
  0.6 25.1 %copy-start.2 = (bf16[3,256,256]{2,1,0:T(8,128)(2,1)S(1)}, bf16[3,256,256]{2,1,0:T(8,128)(2,1)}, u32[]{:S(2)}) copy-start(bf16[3,256,256]{2,1,0:T(8,128)(2,1)} %param.11) | copy-start | bytes 1179652
  2.3 31.9 %collective-permute-start.3 = (bf16[2,4,48,256]{3,2,1,0:T(8,128)(2,1)}, bf16[2,4,48,256]{3,2,1,0:T(8,128)(2,1)S(1)}, u32[]{:S(2)}, u32[]{:S(2)}) collective-permute-start(bf16[2,4,48,256]{3,2,1,0:T(8,128)(2,1)} %slice_bitcast_fusion), channel_id=1, source_target_pairs={{16,0},{32,16},{48,32},{64,48},{80,64},{96,80},{112,96},{128,112},... | collective-permute-start | bytes 589832 | tf_op jit(solution)/shard_map/ppermute | solution.py:24
  17.1 9.1 %copy-start.4 = (bf16[3,3,256,256]{3,2,1,0:T(8,128)(2,1)S(1)}, bf16[3,3,256,256]{3,2,1,0:T(8,128)(2,1)}, u32[]{:S(2)}) copy-start(bf16[3,3,256,256]{3,2,1,0:T(8,128)(2,1)} %param.10) | copy-start | bytes 3538948
  17.1 16.2 %collective-permute-start.2 = (bf16[2,4,48,256]{3,2,1,0:T(8,128)(2,1)}, bf16[2,4,48,256]{3,2,1,0:T(8,128)(2,1)}, u32[]{:S(2)}, u32[]{:S(2)}) collective-permute-start(bf16[2,4,48,256]{3,2,1,0:T(8,128)(2,1)} %slice_bitcast_fusion.1), channel_id=1, source_target_pairs={{0,16},{16,32},{32,48},{48,64},{64,80},{80,96},{96,112},{112,128},... | collective-permute-start | bytes 589832 | tf_op jit(solution)/shard_map/ppermute | solution.py:24
  20.9 19.1 %collective-permute-start = (bf16[4,1,48,512]{3,2,1,0:T(8,128)(2,1)}, bf16[4,1,48,512]{3,2,1,0:T(8,128)(2,1)S(1)}, u32[]{:S(2)}, u32[]{:S(2)}) collective-permute-start(bf16[4,1,48,512]{3,2,1,0:T(8,128)(2,1)} %get-tuple-element.39), channel_id=1, source_target_pairs={{0,2},{2,4},{4,6},{6,8},{8,10},{10,12},{12,14},{1,3},{3,5},{5,7},{... | collective-permute-start | bytes 589832 | tf_op jit(solution)/shard_map/ppermute | solution.py:15
  24.4 15.6 %collective-permute-start.1 = (bf16[4,1,48,512]{3,2,1,0:T(8,128)(2,1)S(1)}, bf16[4,1,48,512]{3,2,1,0:T(8,128)(2,1)}, u32[]{:S(2)}, u32[]{:S(2)}) collective-permute-start(bf16[4,1,48,512]{3,2,1,0:T(8,128)(2,1)S(1)} %get-tuple-element.40), channel_id=1, source_target_pairs={{2,0},{4,2},{6,4},{8,6},{10,8},{12,10},{14,12},{3,1},{5,3},{7,5},{... | collective-permute-start | bytes 589832 | tf_op jit(solution)/shard_map/ppermute | solution.py:16
  27.4 1.0 copy-start.12
  28.6 11.0 %copy-start.8 = (bf16[1,256,256]{1,2,0:T(8,128)(2,1)}, bf16[1,256,256]{1,2,0:T(8,128)(2,1)S(1)}, u32[]{:S(2)}) copy-start(bf16[1,256,256]{1,2,0:T(8,128)(2,1)S(1)} %copy.23) | copy-start | bytes 393220
  28.8 10.9 %copy-start.10 = (bf16[1,256,256]{1,2,0:T(8,128)(2,1)}, bf16[1,256,256]{1,2,0:T(8,128)(2,1)S(1)}, u32[]{:S(2)}) copy-start(bf16[1,256,256]{1,2,0:T(8,128)(2,1)S(1)} %copy.24) | copy-start | bytes 393220
  34.3 11.0 %collective-permute-start.4 = (bf16[2,1,48,512]{3,2,1,0:T(8,128)(2,1)S(1)}, bf16[2,1,48,512]{3,2,1,0:T(8,128)(2,1)S(1)}, u32[]{:S(2)}, u32[]{:S(2)}) collective-permute-start(bf16[2,1,48,512]{3,2,1,0:T(8,128)(2,1)S(1)} %get-tuple-element.50), channel_id=1, source_target_pairs={{0,2},{2,4},{4,6},{6,8},{8,10},{10,12},{12,14},{1,3},{3,5},{5,7},{... | collective-permute-start | bytes 294920 | tf_op jit(solution)/shard_map/ppermute | solution.py:15
  37.8 7.5 %collective-permute-start.5 = (bf16[2,1,48,512]{3,2,1,0:T(8,128)(2,1)S(1)}, bf16[2,1,48,512]{3,2,1,0:T(8,128)(2,1)S(1)}, u32[]{:S(2)}, u32[]{:S(2)}) collective-permute-start(bf16[2,1,48,512]{3,2,1,0:T(8,128)(2,1)S(1)} %get-tuple-element.51), channel_id=1, source_target_pairs={{2,0},{4,2},{6,4},{8,6},{10,8},{12,10},{14,12},{3,1},{5,3},{7,5},{... | collective-permute-start | bytes 294920 | tf_op jit(solution)/shard_map/ppermute | solution.py:16
  39.6 1.0 copy-start.3
  41.7 3.6 %copy-start.1 = (bf16[4,6,48,512]{3,2,1,0:T(8,128)(2,1)}, bf16[4,6,48,512]{3,2,1,0:T(8,128)(2,1)S(1)}, u32[]{:S(2)}) copy-start(bf16[4,6,48,512]{3,2,1,0:T(8,128)(2,1)S(1)} %pad_maximum_fusion) | copy-start | bytes 3538948
  42.9 1.3 copy-start.5
  45.3 0.7 copy-start.6
  45.3 1.2 slice-start
  46.5 0.9 copy-start.9
  46.5 1.0 copy-start.11
  49.8 0.9 slice-start.1
  49.8 1.1 copy-start.7
  52.2 1.4 copy-start.13
where the time goes:
time: 260 us
  blocking collectives  204 us (78%)
  starting transfers between devices  24.7 us (10%)
  local copies, waits for them, and re-layouts  11.3 us (4%)
  matrix products  9.46 us (4%)
  waiting for transfers between devices  4.52 us (2%)
  other arithmetic  4.02 us (2%)
    psum x1, blocking collectives, local(): lax.psum((spatial_term * grad_scale, temporal_term * grad_scale), ('tm',...  204 us
    ppermute x2, starting transfers between devices, from_behind(): return lax.ppermute(block, axis, route)  15.2 us
    ppermute x2, starting transfers between devices, extended(): before = lax.ppermute(last, axis, up)  6.97 us
    unnamed x71, local copies, waits for them, and re-layouts  6.45 us
  transfers between devices with their start and end apart: 6, of which 1 were waited for; matrix products, arithmetic and copies ran while one was open for 4% of the time, Pallas kernels for 0%

commit v1 on v0

--- a/solution.py
+++ b/solution.py
@@ -132,7 +132,7 @@
         frame_stack, upstream.reshape(-1, channels), contract, preferred_element_type=jnp.float32
     )
     spatial_sum, temporal_sum = lax.psum(
-        (spatial_term * grad_scale, temporal_term * grad_scale), ("tm", "height", "dp")
+        lax.psum((spatial_term * grad_scale, temporal_term * grad_scale), ("height", "dp")), "tm"
     )
     spatial_grad = spatial_sum.astype(jnp.bfloat16).reshape(3, 3, channels, channels)
     temporal_grad = temporal_sum.astype(jnp.bfloat16).reshape(3, channels, channels)

time: 260 us -> 672 us (2.58)
  the two profiles are of different devices: /device:TPU:2 before, /device:TPU:24 now
where the time goes in v1:
time: 672 us; the launch traced here: 671 us
  waiting for transfers between devices  295 us (44%)
  blocking collectives  281 us (42%)
  starting transfers between devices  40.6 us (6%)
  local copies, waits for them, and re-layouts  24.9 us (4%)
  between operations  14.8 us (2%)
  matrix products  10.9 us (2%)
    psum x1, waiting for transfers between devices, local(): lax.psum((spatial_term * grad_scale, temporal_term * grad_scale), ('heigh...  287 us
    psum x1, blocking collectives, local(): lax.psum(lax.psum((spatial_term * grad_scale, temporal_term * grad_scale)...  281 us
    ppermute x2, starting transfers between devices, extended(): before = lax.ppermute(last, axis, up)  30.1 us
    unnamed x85, local copies, waits for them, and re-layouts  18.8 us
  transfers between devices with their start and end apart: 7, of which 2 were waited for; matrix products, arithmetic and copies ran while one was open for 5% of the time, Pallas kernels for 0%

profile of v1, /device:TPU:24, one launch (start us, length us, event | category | flops | bytes accessed | tf_op | source)
XLA Modules:
  0.0 671.0 jit_solution(3658747555205661563)
XLA Ops:
  7.2 1.7 slice_bitcast_fusion
  8.9 1.3 collective-permute-start.3
  10.2 1.6 slice_bitcast_fusion.1
  11.8 5.4 collective-permute-start.2
  17.2 1.8 pad_maximum_fusion.8
  19.0 15.4 %collective-permute-start = (bf16[4,1,48,512]{3,2,1,0:T(8,128)(2,1)}, bf16[4,1,48,512]{3,2,1,0:T(8,128)(2,1)}, u32[]{:S(2)}, u32[]{:S(2)}) collective-permute-start(bf16[4,1,48,512]{3,2,1,0:T(8,128)(2,1)} %get-tuple-element.41), channel_id=1, source_target_pairs={{0,2},{2,4},{4,6},{6,8},{8,10},{10,12},{12,14},{1,3},{3,5},{5,7},{... | collective-permute-start | bytes 589832 | tf_op jit(solution)/shard_map/ppermute | solution.py:15
  34.4 1.9 collective-permute-start.1
  36.3 0.6 fusion.93
  36.9 0.8 fusion.94
  37.7 0.2 fusion.75
  37.9 0.2 convolution_add_fusion.2
  38.1 0.8 fusion.92
  38.9 1.7 copy.33
  40.6 1.7 copy.32
  42.2 0.8 copy.31
  43.0 0.8 copy.30
  43.8 0.8 copy.29
  44.5 0.7 copy.28
  45.3 0.7 copy.27
  46.1 0.1 copy.25
  46.3 0.9 bitcast_dynamic-update-slice_fusion.6
  47.2 0.9 bitcast_dynamic-update-slice_fusion.5
  48.1 0.9 bitcast_dynamic-update-slice_fusion.4
  49.1 1.1 copy-done.19
  50.2 1.0 copy.22
  51.2 1.0 copy.23
  52.3 1.0 copy.24
  53.4 1.0 constant_dynamic-update-slice_fusion.1
  54.4 14.8 %collective-permute-start.4 = (bf16[2,1,48,512]{3,2,1,0:T(8,128)(2,1)S(1)}, bf16[2,1,48,512]{3,2,1,0:T(8,128)(2,1)S(1)}, u32[]{:S(2)}, u32[]{:S(2)}) collective-permute-start(bf16[2,1,48,512]{3,2,1,0:T(8,128)(2,1)S(1)} %get-tuple-element.52), channel_id=1, source_target_pairs={{0,2},{2,4},{4,6},{6,8},{8,10},{10,12},{12,14},{1,3},{3,5},{5,7},{... | collective-permute-start | bytes 294920 | tf_op jit(solution)/shard_map/ppermute | solution.py:15
  69.2 1.9 collective-permute-start.5
  71.2 0.5 fusion.15
  71.7 0.4 copy-done.12
  72.0 0.2 fusion.71
  72.4 0.3 copy-done.3
  72.7 1.1 pad_maximum_fusion
  73.8 0.4 fusion.9
  74.2 0.1 fusion.51
  74.4 0.1 fusion.52
  74.5 0.1 fusion.53
  74.6 0.1 fusion.54
  74.8 0.1 fusion.55
  74.9 0.1 fusion.56
  75.0 2.6 convolution_multiply_fusion
  77.6 1.1 convolution_convert_fusion
  78.7 7.9 %collective-permute-done.5 = bf16[2,1,48,512]{3,2,1,0:T(8,128)(2,1)S(1)} collective-permute-done((bf16[2,1,48,512]{3,2,1,0:T(8,128)(2,1)S(1)}, bf16[2,1,48,512]{3,2,1,0:T(8,128)(2,1)S(1)}, u32[]{:S(2)}, u32[]{:S(2)}) %collective-permute-start.5) | collective-permute-done | bytes 98336 | tf_op jit(solution)/shard_map/ppermute | solution.py:16
  86.7 0.2 fusion.46
  87.0 0.2 fusion.78
  87.2 0.2 convolution_add_fusion.4
  87.5 0.4 copy-done.14
  88.0 0.3 fusion.64
  88.7 0.6 convolution_convert_fusion.1
  89.4 0.2 slice-done.1
  89.6 0.2 copy-done.6
  89.9 1.4 convolution_multiply_fusion.1
  91.3 0.2 fusion.32
  91.5 0.3 fusion.42
  91.8 0.1 slice_dynamic-update-slice_fusion.5
  92.0 0.1 slice_dynamic-update-slice_fusion.3
  92.2 0.1 slice_dynamic-update-slice_fusion.1
  92.4 0.7 copy-done.7
  93.2 1.2 fusion.4
  94.5 1.9 fusion.5
  96.4 287.2 %all-reduce.8.cloned.1.call-done = (f32[2304,256]{1,0:T(8,128)}, f32[768,256]{1,0:T(8,128)}) async-done(((f32[2304,256]{1,0:T(8,128)}, f32[768,256]{1,0:T(8,128)}), (f32[2304,256]{1,0:T(8,128)}, f32[768,256]{1,0:T(8,128)})) %all-reduce.8.cloned.1.call-update) | async-done | bytes 3145744 | tf_op jit(solution)/shard_map/psum | solution.py:135
  383.6 280.6 %all-reduce.9 = (bf16[2304,256]{1,0:T(8,128)(2,1)}, bf16[768,256]{1,0:T(8,128)(2,1)}) all-reduce(f32[2304,256]{1,0:T(8,128)} %get-tuple-element.30, f32[768,256]{1,0:T(8,128)} %get-tuple-element.31), channel_id=1, replica_groups=mesh['tm'=32,'height'=8,'dp'=2] {'tm'}, use_global_device_ids=true, to_apply=%region_1.2 | all-reduce | flops 786432 | bytes 4718592 | tf_op jit(solution)/shard_map/psum | solution.py:134
  (85 shorter events, 1.5 us)
Async XLA Ops:
  7.2 29.1 %copy-start = (bf16[1,4,4,48,256]{4,3,2,1,0:T(8,128)(2,1)S(1)}, bf16[1,4,4,48,256]{4,3,2,1,0:T(8,128)(2,1)}, u32[]{:S(2)}) copy-start(bf16[1,4,4,48,256]{4,3,2,1,0:T(8,128)(2,1)} %param.9) | copy-start | bytes 1179652
  7.2 29.8 %copy-start.2 = (bf16[3,256,256]{2,1,0:T(8,128)(2,1)S(1)}, bf16[3,256,256]{2,1,0:T(8,128)(2,1)}, u32[]{:S(2)}) copy-start(bf16[3,256,256]{2,1,0:T(8,128)(2,1)} %param.11) | copy-start | bytes 1179652
  7.2 376.4 %all-reduce.8.cloned.1.call-start = ((), (), s32[]{:S(2)}) async-start(), calls=%async_computation | async-start | bytes 6291456 | tf_op jit(solution)/shard_map/psum | solution.py:135
  8.9 45.4 %collective-permute-start.3 = (bf16[2,4,48,256]{3,2,1,0:T(8,128)(2,1)}, bf16[2,4,48,256]{3,2,1,0:T(8,128)(2,1)S(1)}, u32[]{:S(2)}, u32[]{:S(2)}) collective-permute-start(bf16[2,4,48,256]{3,2,1,0:T(8,128)(2,1)} %slice_bitcast_fusion), channel_id=1, source_target_pairs={{16,0},{32,16},{48,32},{64,48},{80,64},{96,80},{112,96},{128,112},... | collective-permute-start | bytes 589832 | tf_op jit(solution)/shard_map/ppermute | solution.py:24
  11.8 26.3 %copy-start.4 = (bf16[3,3,256,256]{3,2,1,0:T(8,128)(2,1)S(1)}, bf16[3,3,256,256]{3,2,1,0:T(8,128)(2,1)}, u32[]{:S(2)}) copy-start(bf16[3,3,256,256]{3,2,1,0:T(8,128)(2,1)} %param.10) | copy-start | bytes 3538948
  11.8 41.5 %collective-permute-start.2 = (bf16[2,4,48,256]{3,2,1,0:T(8,128)(2,1)}, bf16[2,4,48,256]{3,2,1,0:T(8,128)(2,1)}, u32[]{:S(2)}, u32[]{:S(2)}) collective-permute-start(bf16[2,4,48,256]{3,2,1,0:T(8,128)(2,1)} %slice_bitcast_fusion.1), channel_id=1, source_target_pairs={{0,16},{16,32},{32,48},{48,64},{64,80},{80,96},{96,112},{112,128},... | collective-permute-start | bytes 589832 | tf_op jit(solution)/shard_map/ppermute | solution.py:24
  19.0 53.4 %collective-permute-start = (bf16[4,1,48,512]{3,2,1,0:T(8,128)(2,1)}, bf16[4,1,48,512]{3,2,1,0:T(8,128)(2,1)}, u32[]{:S(2)}, u32[]{:S(2)}) collective-permute-start(bf16[4,1,48,512]{3,2,1,0:T(8,128)(2,1)} %get-tuple-element.41), channel_id=1, source_target_pairs={{0,2},{2,4},{4,6},{6,8},{8,10},{10,12},{12,14},{1,3},{3,5},{5,7},{... | collective-permute-start | bytes 589832 | tf_op jit(solution)/shard_map/ppermute | solution.py:15
  34.4 38.0 %collective-permute-start.1 = (bf16[4,1,48,512]{3,2,1,0:T(8,128)(2,1)}, bf16[4,1,48,512]{3,2,1,0:T(8,128)(2,1)}, u32[]{:S(2)}, u32[]{:S(2)}) collective-permute-start(bf16[4,1,48,512]{3,2,1,0:T(8,128)(2,1)} %get-tuple-element.42), channel_id=1, source_target_pairs={{2,0},{4,2},{6,4},{8,6},{10,8},{12,10},{14,12},{3,1},{5,3},{7,5},{... | collective-permute-start | bytes 589832 | tf_op jit(solution)/shard_map/ppermute | solution.py:16
  43.0 6.1 copy-start.9
  43.8 5.4 copy-start.8
  44.5 4.5 copy-start.10
  45.3 3.8 copy-start.11
  49.1 1.1 copy-start.19
  51.2 20.4 %copy-start.13 = (bf16[1,256,256]{1,2,0:T(8,128)(2,1)}, bf16[1,256,256]{1,2,0:T(8,128)(2,1)S(1)}, u32[]{:S(2)}) copy-start(bf16[1,256,256]{1,2,0:T(8,128)(2,1)S(1)} %copy.22) | copy-start | bytes 393220
  52.3 19.4 %copy-start.15 = (bf16[1,256,256]{1,2,0:T(8,128)(2,1)}, bf16[1,256,256]{1,2,0:T(8,128)(2,1)S(1)}, u32[]{:S(2)}) copy-start(bf16[1,256,256]{1,2,0:T(8,128)(2,1)S(1)} %copy.23) | copy-start | bytes 393220
  53.3 18.3 %copy-start.17 = (bf16[1,256,256]{1,2,0:T(8,128)(2,1)}, bf16[1,256,256]{1,2,0:T(8,128)(2,1)S(1)}, u32[]{:S(2)}) copy-start(bf16[1,256,256]{1,2,0:T(8,128)(2,1)S(1)} %copy.24) | copy-start | bytes 393220
  54.4 24.3 %collective-permute-start.4 = (bf16[2,1,48,512]{3,2,1,0:T(8,128)(2,1)S(1)}, bf16[2,1,48,512]{3,2,1,0:T(8,128)(2,1)S(1)}, u32[]{:S(2)}, u32[]{:S(2)}) collective-permute-start(bf16[2,1,48,512]{3,2,1,0:T(8,128)(2,1)S(1)} %get-tuple-element.52), channel_id=1, source_target_pairs={{0,2},{2,4},{4,6},{6,8},{8,10},{10,12},{12,14},{1,3},{3,5},{5,7},{... | collective-permute-start | bytes 294920 | tf_op jit(solution)/shard_map/ppermute | solution.py:15
  69.2 17.4 %collective-permute-start.5 = (bf16[2,1,48,512]{3,2,1,0:T(8,128)(2,1)S(1)}, bf16[2,1,48,512]{3,2,1,0:T(8,128)(2,1)S(1)}, u32[]{:S(2)}, u32[]{:S(2)}) collective-permute-start(bf16[2,1,48,512]{3,2,1,0:T(8,128)(2,1)S(1)} %get-tuple-element.53), channel_id=1, source_target_pairs={{2,0},{4,2},{6,4},{8,6},{10,8},{12,10},{14,12},{3,1},{5,3},{7,5},{... | collective-permute-start | bytes 294920 | tf_op jit(solution)/shard_map/ppermute | solution.py:16
  71.2 0.9 copy-start.12
  71.7 1.0 copy-start.3
  73.8 4.9 copy-start.1
  78.7 8.2 %copy-start.5 = (bf16[768,256]{1,0:T(8,128)(2,1)}, bf16[768,256]{1,0:T(8,128)(2,1)S(1)}, u32[]{:S(2)}) copy-start(bf16[768,256]{1,0:T(8,128)(2,1)S(1)} %convolution_convert_fusion) | copy-start | bytes 1179652
  78.7 8.2 %slice-start = ((bf16[4,6,48,512]{3,2,1,0:T(8,128)(2,1)}), bf16[4,6,48,256]{3,2,1,0:T(8,128)(2,1)S(1)}, s32[]{:S(2)}) async-start(bf16[4,6,48,512]{3,2,1,0:T(8,128)(2,1)} %copy-done.1), calls=%async_computation.1 | async-start | bytes 1179648 | tf_op jit(solution)/shard_map/slice | solution.py:108
  86.9 0.9 copy-start.14
  87.0 1.0 copy-start.16
  87.0 1.0 copy-start.18
  88.7 0.9 slice-start.1
  88.7 1.1 copy-start.6
  92.2 1.0 copy-start.7
  93.2 1.3 copy-start.20
Sparse Core Ops, SparseCore 0:
  91.4 292.1 all-reduce.7
